TPU v7x, 256 devices: a whole 4x4x8 slice. The times are simulated.
256 devices in a mesh: ctx: 16 (over z, core), head: 4 (over y), rep: 4 (over x).
Axes of the slice: x: 4, y: 4, z: 8, core: 2. Of those that a mesh axis runs over, the one named last changes fastest.
Arguments:
- kv_cache: float32 [8, 2, 4096, 8, 128], P('head', None, 'ctx', 'rep'), may hold values from -8 to 8
- prefill_q: float32 [8, 256, 64, 128], P('head', 'ctx', 'rep'), may hold values from -512 to 512
- decode_q: float32 [8, 64, 4, 64, 128], P(None, ('ctx', 'rep'), None, 'head'), may hold values from -512 to 512
- decode_kv: float32 [8, 64, 4, 2, 8, 128], P(None, ('ctx', 'rep'), None, None, 'head'), may hold values from -12 to 12
- lengths: int32 [8], replicated, may hold values from 1024 to 4096, as said below
- row_length: int32 [8, 64], P(None, ('ctx', 'rep')), may hold values from 2 to 4096, as said below
Outputs:
- prefill_out: float32 [8, 256, 64, 128], P('head', 'ctx', 'rep')
- decode_out: float32 [8, 64, 4, 64, 128], P(None, ('ctx', 'rep'), None, 'head')
Inputs may be any that keep to these rules, and one draw needn't show every extreme that they name: `lengths`: multiples of 128; some request has length 4096. `row_length`: a row reads at most its request's length; every request has a row that reads its whole length.
All inputs are finite; a program needn't handle non-finite values.
Results may differ from a plain program's by a relative error of at most 0.0003.
Values sent between devices are 32-bit elements; how exact they have to be, the bound alone decides.
A program may use at most 128 MiB of HBM per device.

v0:
```python
import functools
import math

import jax
import jax.numpy as jnp
from jax import lax
from jax.experimental import pallas as pl
from jax.experimental.pallas import tpu as pltpu
from jax.sharding import PartitionSpec as P

MESH = pl.DeviceIdType.MESH
NEG_FILL = -1e30
F32 = jnp.float32
BF16 = jnp.bfloat16
CHIPS = 8
NQ = 1024
HALF = 512
BLK = 256
QC = 256


def split2(x):
    hi = x.astype(BF16)
    return hi, (x - hi.astype(F32)).astype(BF16)


def split3(x):
    hi = x.astype(BF16)
    rest = x - hi.astype(F32)
    mid = rest.astype(BF16)
    return hi, mid, (rest - mid.astype(F32)).astype(BF16)


def key_terms(k):
    hi, mid, lo = split3(k)
    return jnp.concatenate([hi, hi, mid, mid, hi, lo], axis=1)


def query_terms(q):
    hi, mid, lo = split3(q)
    return jnp.concatenate([hi, mid, hi, mid, lo, hi], axis=1)


def value_terms(v):
    hi, lo = split2(v.T)
    return jnp.concatenate([hi, lo], axis=0)


def dot_nt(a, b):
    return lax.dot_general(a, b, (((1,), (1,)), ((), ())), preferred_element_type=F32)


def weighted(v2, p):
    hi, lo = split2(p)
    both = jnp.dot(v2, hi, preferred_element_type=F32) + jnp.dot(v2, lo, preferred_element_type=F32)
    return both[:128] + both[128:]


def kernel(
    scale,
    span,
    len_ref,
    rl_ref,
    kv_ref,
    pq_ref,
    dq_ref,
    dkv_ref,
    po_ref,
    do_ref,
    raw,
    sendb,
    kvb,
    qb,
    lb,
    db,
    q6,
    k6,
    v2b,
    lim,
    m_ref,
    l_ref,
    acc,
    ob,
    sem_local,
    sem_pq_s,
    sem_pq_r,
    sem_dq_s,
    sem_dq_r,
    sem_kp_s,
    sem_kf_s,
    sem_kx_s,
    sem_k_r,
    sem_po_s,
    sem_po_r,
    sem_do_s,
    sem_do_r,
):
    c = lax.axis_index("ctx")
    y = lax.axis_index("head")
    x = lax.axis_index("rep")
    z = c // 2
    core = c % 2

    def dest(t):
        even = (z + t) % 2 == 0
        return lax.rem(jnp.where(even, z + t, z - t + CHIPS), CHIPS)

    def source_of(chip, t):
        return lax.rem(jnp.where(chip % 2 == 0, chip - t + CHIPS, chip + t), CHIPS)

    mate = z + 1 - 2 * (z % 2)
    pair = z // 2
    own_i = pair // 2
    own_j = pair % 2
    diag = x == y

    load = pltpu.make_async_copy(kv_ref, raw, sem_local.at[0])
    load.start()

    barrier = pltpu.get_barrier_semaphore()

    def greet(ctx, head, rep):
        pl.semaphore_signal(barrier, inc=1, device_id=(ctx, head, rep), device_id_type=MESH)

    greet(2 * z + 1 - core, y, x)
    greet(2 * mate + core, y, x)
    count = 2
    for t in range(4):
        to_c = 2 * dest(t) + core
        from_c = 2 * source_of(z, t) + core
        if t:
            greet(to_c, y, x)
            greet(from_c, y, x)
            count += 2
        for g in range(4):
            if t:
                greet(to_c, g, y)
                greet(from_c, x, g)
            else:

                @pl.when(jnp.logical_not((y == g) & diag))
                def _():
                    greet(to_c, g, y)
                    greet(from_c, x, g)

            count += 2

    load.wait()
    for i in range(2):
        for s in range(2):
            for j in range(2):
                sendb[2 * i + j, s] = raw[i, s, pl.ds(j, BLK, stride=2), :]

    pl.semaphore_wait(barrier, jnp.where(diag, count - 2, count))

    def pq_copy(t):
        zt = dest(t)
        p = zt // 2
        src = pq_ref.at[p // 2, :, pl.ds(pl.multiple_of(8 * (p % 2), 8), 8), :]
        dst = qb.at[pl.ds(16 * t, 16)]
        if t == 0:
            return pltpu.make_async_copy(src, dst, sem_pq_r.at[0])
        return pltpu.make_async_remote_copy(
            src, dst, sem_pq_s.at[t], sem_pq_r.at[t], device_id=(2 * zt + core, y, x), device_id_type=MESH
        )

    def dq_parts(t, g):
        p = dest(t) // 2
        req = 2 * g + p // 2
        slot = 4 * t + x
        return (
            (dq_ref.at[req, :, pl.ds(pl.multiple_of(8 * (p % 2), 8), 8), :], qb.at[pl.ds(64 + 4 * slot, 4)]),
            (dkv_ref.at[req], db.at[slot]),
            (rl_ref.at[req], lb.at[slot]),
        )

    def dq_remote(t, g, n, part):
        return pltpu.make_async_remote_copy(
            part[0],
            part[1],
            sem_dq_s.at[4 * t + g, n],
            sem_dq_r.at[4 * t + x, n],
            device_id=(2 * dest(t) + core, g, y),
            device_id_type=MESH,
        )

    def dq_start(t, g):
        for n, part in enumerate(dq_parts(t, g)):
            if t:
                dq_remote(t, g, n, part).start()
            else:
                mine = (y == g) & diag

                @pl.when(mine)
                def _():
                    pltpu.make_async_copy(part[0], part[1], sem_dq_r.at[4 * t + x, n]).start()

                @pl.when(jnp.logical_not(mine))
                def _():
                    dq_remote(t, g, n, part).start()

    def dq_wait_send(t, g):
        for n, part in enumerate(dq_parts(t, g)):
            if t:
                dq_remote(t, g, n, part).wait_send()
            else:

                @pl.when(jnp.logical_not((y == g) & diag))
                def _():
                    dq_remote(t, g, n, part).wait_send()

    def kv_primary(t):
        zt = dest(t)
        return pltpu.make_async_remote_copy(
            sendb.at[zt // 2],
            kvb.at[t],
            sem_kp_s.at[t],
            sem_k_r.at[t],
            device_id=(2 * zt + core, y, x),
            device_id_type=MESH,
        )

    def kv_forward(t):
        return pltpu.make_async_remote_copy(
            kvb.at[t],
            kvb.at[t + 4],
            sem_kf_s.at[t],
            sem_k_r.at[t + 4],
            device_id=(2 * mate + core, y, x),
            device_id_type=MESH,
        )

    def kv_cross(u):
        return pltpu.make_async_remote_copy(
            kvb.at[u],
            kvb.at[u + 8],
            sem_kx_s.at[u],
            sem_k_r.at[u + 8],
            device_id=(2 * z + 1 - core, y, x),
            device_id_type=MESH,
        )

    keep = pltpu.make_async_copy(sendb.at[pair], kvb.at[0], sem_k_r.at[0])
    keep.start()
    for t in (3, 2, 1, 0):
        pq_copy(t).start()
        for g in range(4):
            dq_start(t, g)
    for t in (3, 2, 1):
        kv_primary(t).start()

    def arrive(u):
        pltpu.make_async_copy(kvb.at[u], kvb.at[u], sem_k_r.at[u]).wait()

        @pl.when(u < 4)
        def _():
            kv_forward(u).start()

        @pl.when(u < 8)
        def _():
            kv_cross(u).start()

    arrive(jnp.int32(0))

    own_len = len_ref[2 * y + own_i]
    lane = lax.broadcasted_iota(jnp.int32, (1, 128), 1)
    for t in range(4):
        first = own_len - (span - 1) + 16 * (2 * source_of(z, t) + core)
        lim[:, pl.ds(128 * t, 128)] = first + lane // 8

    for t in range(4):
        part = qb.at[pl.ds(16 * t, 16)]
        pltpu.make_async_copy(part, part, sem_pq_r.at[t]).wait()

    @pl.loop(0, 16)
    def _(s):
        part = qb.at[pl.ds(64 + 4 * s, 4)]
        pltpu.make_async_copy(part, part, sem_dq_r.at[s, 0]).wait()
        pltpu.make_async_copy(db.at[s], db.at[s], sem_dq_r.at[s, 1]).wait()
        pltpu.make_async_copy(lb.at[s], lb.at[s], sem_dq_r.at[s, 2]).wait()

    for v in range(4):
        row = jnp.where(
            lane < 64,
            jnp.where(lane < 32, lb[4 * v], lb[4 * v + 1]),
            jnp.where(lane < 96, lb[4 * v + 2], lb[4 * v + 3]),
        )
        lim[:, pl.ds(HALF + 128 * v, 128)] = row

    @pl.loop(0, NQ // 128)
    def _(n):
        q = qb[pl.ds(16 * n, 16)].reshape(128, 128) * scale
        q6[pl.ds(pl.multiple_of(128 * n, 128), 128), :] = query_terms(q)

    m_ref[:, :HALF] = jnp.full((1, HALF), NEG_FILL, F32)
    l_ref[:, :HALF] = jnp.zeros((1, HALF), F32)
    acc[:, :HALF] = jnp.zeros((128, HALF), F32)
    drafts = db[...].reshape(64, 4, 128)
    dk = jnp.where(own_j == 0, drafts[:, 0], drafts[:, 1])
    dv = jnp.where(own_j == 0, drafts[:, 2], drafts[:, 3])
    s = dot_nt(key_terms(dk), q6[pl.ds(HALF, HALF), :])
    key_id = lax.broadcasted_iota(jnp.int32, (64, HALF), 0)
    query_id = lax.broadcasted_iota(jnp.int32, (64, HALF), 1) // 8
    s = jnp.where((key_id // 4 == query_id // 4) & (key_id <= query_id), s, NEG_FILL)
    top = jnp.max(s, axis=0, keepdims=True)
    p = jnp.exp2(s - top)
    m_ref[:, HALF:] = top
    l_ref[:, HALF:] = jnp.sum(p, axis=0, keepdims=True)
    acc[:, HALF:] = weighted(value_terms(dv), p)

    def order(n):
        return n // 4 + (n % 2) * 8 + ((n // 2) % 2) * 4

    @pl.loop(0, 16)
    def _(n):
        u = order(n)

        @pl.when(n < 15)
        def _():
            arrive(order(n + 1))

        t = u % 4
        chip = jnp.where((u // 4) % 2 == 0, z, mate)
        owner = jnp.where(u < 8, core, 1 - core)
        first = BLK * (2 * source_of(chip, t) + owner)
        k6[...] = key_terms(kvb[u, 0])
        v2b[...] = value_terms(kvb[u, 1])
        for qc in range(NQ // QC):
            cols = pl.ds(QC * qc, QC)
            s = dot_nt(k6[...], q6[pl.ds(QC * qc, QC), :])
            place = lax.broadcasted_iota(jnp.int32, (BLK, QC), 0)
            s = jnp.where(place < lim[:, cols] - first, s, NEG_FILL)
            old = m_ref[:, cols]
            top = jnp.maximum(old, jnp.max(s, axis=0, keepdims=True))
            fade = jnp.exp2(old - top)
            p = jnp.exp2(s - top)
            m_ref[:, cols] = top
            l_ref[:, cols] = l_ref[:, cols] * fade + jnp.sum(p, axis=0, keepdims=True)
            acc[:, cols] = acc[:, cols] * fade + weighted(v2b[...], p)

    rows_j = pl.ds(pl.multiple_of(8 * own_j, 8), 8)

    def po_copy(t):
        src = ob.at[pl.ds(16 * t, 16)]
        dst = po_ref.at[own_i, :, rows_j, :]
        if t == 0:
            return pltpu.make_async_copy(src, dst, sem_po_r.at[0])
        return pltpu.make_async_remote_copy(
            src,
            dst,
            sem_po_s.at[t],
            sem_po_r.at[t],
            device_id=(2 * source_of(z, t) + core, y, x),
            device_id_type=MESH,
        )

    def do_ends(t, r):
        return ob.at[pl.ds(64 + 16 * t + 4 * r, 4)], do_ref.at[2 * y + own_i, :, rows_j, :]

    def do_remote(t, r):
        src, dst = do_ends(t, r)
        return pltpu.make_async_remote_copy(
            src,
            dst,
            sem_do_s.at[4 * t + r],
            sem_do_r.at[4 * t + y],
            device_id=(2 * source_of(z, t) + core, x, r),
            device_id_type=MESH,
        )

    def do_start(t, r):
        if t:
            do_remote(t, r).start()
            return
        mine = (x == r) & diag

        @pl.when(mine)
        def _():
            src, dst = do_ends(t, r)
            pltpu.make_async_copy(src, dst, sem_do_r.at[4 * t + y]).start()

        @pl.when(jnp.logical_not(mine))
        def _():
            do_remote(t, r).start()

    for qc in (3, 1, 2, 0):
        cols = pl.ds(QC * qc, QC)
        out = acc[:, cols] * (1.0 / l_ref[:, cols])
        ob[pl.ds(32 * qc, 32)] = out.T.reshape(32, 8, 128)
        for t in (2 * (qc % 2) + 1, 2 * (qc % 2)):
            if qc < 2:
                po_copy(t).start()
            else:
                for r in range(4):
                    do_start(t, r)

    for t in range(1, 4):
        pq_copy(t).wait_send()
        kv_primary(t).wait_send()
    for t in range(4):
        for g in range(4):
            dq_wait_send(t, g)
        kv_forward(t).wait_send()
    for u in range(8):
        kv_cross(u).wait_send()
    for t in range(4):
        if t:
            po_copy(t).wait_send()
        p = dest(t) // 2
        rows = pl.ds(pl.multiple_of(8 * (p % 2), 8), 8)
        got = po_ref.at[p // 2, :, rows, :]
        pltpu.make_async_copy(got, got, sem_po_r.at[t]).wait()
        for g in range(4):
            if t:
                do_remote(t, g).wait_send()
            else:

                @pl.when(jnp.logical_not((x == g) & diag))
                def _():
                    do_remote(t, g).wait_send()

            got = do_ref.at[2 * g + p // 2, :, rows, :]
            pltpu.make_async_copy(got, got, sem_do_r.at[4 * t + g]).wait()


def on_device(kv_cache, prefill_q, decode_q, decode_kv, lengths, row_length):
    head_dim = prefill_q.shape[-1]
    span = prefill_q.shape[1] * lax.axis_size("ctx")
    scale = math.log2(math.e) / math.sqrt(head_dim)
    limits = jnp.broadcast_to(row_length[:, :, None], (8, 1, 128))
    hbm = pl.BlockSpec(memory_space=pltpu.MemorySpace.HBM)
    dma = pltpu.SemaphoreType.DMA
    prefill_out, decode_out = pl.pallas_call(
        functools.partial(kernel, scale, span),
        out_shape=(
            jax.ShapeDtypeStruct((2, 16, 16, 128), F32),
            jax.ShapeDtypeStruct((8, 4, 16, 128), F32),
        ),
        in_specs=[pl.BlockSpec(memory_space=pltpu.SMEM)] + [hbm] * 5,
        out_specs=(hbm, hbm),
        scratch_shapes=[
            pltpu.VMEM((2, 2, 512, 128), F32),
            pltpu.VMEM((4, 2, BLK, 128), F32),
            pltpu.VMEM((16, 2, BLK, 128), F32),
            pltpu.VMEM((128, 8, 128), F32),
            pltpu.VMEM((16, 1, 128), jnp.int32),
            pltpu.VMEM((16, 16, 128), F32),
            pltpu.VMEM((NQ, 768), BF16),
            pltpu.VMEM((BLK, 768), BF16),
            pltpu.VMEM((256, BLK), BF16),
            pltpu.VMEM((1, NQ), jnp.int32),
            pltpu.VMEM((1, NQ), F32),
            pltpu.VMEM((1, NQ), F32),
            pltpu.VMEM((128, NQ), F32),
            pltpu.VMEM((128, 8, 128), F32),
            dma((1,)),
            dma((4,)),
            dma((4,)),
            dma((16, 3)),
            dma((16, 3)),
            dma((4,)),
            dma((4,)),
            dma((8,)),
            dma((16,)),
            dma((4,)),
            dma((4,)),
            dma((16,)),
            dma((16,)),
        ],
        compiler_params=pltpu.CompilerParams(
            collective_id=0, has_side_effects=True, vmem_limit_bytes=56 * 1024 * 1024
        ),
    )(
        lengths,
        limits,
        kv_cache.reshape(2, 2, 512, 128),
        prefill_q,
        decode_q.reshape(8, 4, 16, 128),
        decode_kv.reshape(8, 16, 128),
    )
    return prefill_out, decode_out.reshape(decode_q.shape)


def solution(mesh):
    in_specs = (
        P("head", None, "ctx", "rep", None),
        P("head", "ctx", "rep", None),
        P(None, ("ctx", "rep"), None, "head", None),
        P(None, ("ctx", "rep"), None, None, "head", None),
        P(),
        P(None, ("ctx", "rep")),
    )
    out_specs = (P("head", "ctx", "rep", None), P(None, ("ctx", "rep"), None, "head", None))
    return jax.shard_map(
        on_device, mesh=mesh, in_specs=in_specs, out_specs=out_specs, check_vma=False
    )
```

profile of v0, /device:TPU:24, one launch (start us, length us, event | category | flops | bytes accessed | tf_op | source)
XLA Modules:
  0.0 104.4 jit_solution(16814773574487076926)
XLA Ops:
  0.6 0.0 copy-start.1
  0.6 0.6 copy-done.1
  1.3 0.7 broadcast_in_dim.9.rl_ref
  2.0 100.0 %shard_map.77 = (f32[2,16,16,128]{3,2,1,0:T(8,128)}, f32[8,4,16,128]{3,2,1,0:T(8,128)}) custom-call(s32[8]{0:T(128)} %len_ref.1, s32[8,1,128]{2,1,0:T(1,128)} %broadcast_in_dim.9.rl_ref, f32[2,2,512,128]{3,2,1,0:T(8,128)} %bitcast.7, f32[2,16,16,128]{3,2,1,0:T(8,128)} %pq_ref.1, f32[8,4,16,128]{3,2,1,0:T(8,128)} %bitcast.9, f32[8,16,128]{2,1,0:T(8,128)} %bitcast.10), custom_call_target="tpu_custom_call" | custom-call | tf_op jit(solution)/shard_map/pallas_call | solution.py:433
  102.0 0.0 copy-start
  102.0 1.7 %copy.11 = f32[2,16,16,128]{3,2,1,0:T(8,128)} copy(f32[2,16,16,128]{3,2,1,0:T(8,128)} %get-tuple-element.10) | data formatting | bytes 524288
  103.7 0.0 copy-done
  103.7 0.7 copy.12
Async XLA Ops:
  0.6 0.7 copy-start.1
  102.0 1.7 %copy-start = (f32[8,4,16,128]{3,2,1,0:T(8,128)S(1)}, f32[8,4,16,128]{3,2,1,0:T(8,128)}, u32[]{:S(2)}) copy-start(f32[8,4,16,128]{3,2,1,0:T(8,128)} %get-tuple-element.5) | copy-start | bytes 786436
where the time goes:
time: 105 us; the launch traced here: 104 us
  Pallas kernels  100 us (95%)
  local copies, waits for them, and re-layouts  3.73 us (4%)
    pallas_call x1, Pallas kernels, on_device(): pl.pallas_call(functools.partial(kernel, scale, span), out_shape=(jax.Sha...  100 us
    unnamed x6, local copies, waits for them, and re-layouts  3.07 us

commit v1 on v0

--- a/solution.py
+++ b/solution.py
@@ -16,7 +16,10 @@
 NQ = 1024
 HALF = 512
 BLK = 256
-QC = 256
+QC = 512
+PIECES = 2
+PIECE = BLK // PIECES
+AHEAD = 1
 
 
 def split2(x):
@@ -70,6 +73,12 @@
     raw,
     sendb,
     kvb,
+    dkv,
+    dsend,
+    rlb,
+    rq,
+    rd,
+    rr,
     qb,
     lb,
     db,
@@ -82,6 +91,8 @@
     acc,
     ob,
     sem_local,
+    sem_y_s,
+    sem_y_r,
     sem_pq_s,
     sem_pq_r,
     sem_dq_s,
@@ -116,6 +127,8 @@
 
     load = pltpu.make_async_copy(kv_ref, raw, sem_local.at[0])
     load.start()
+    load_d = pltpu.make_async_copy(dkv_ref, dkv, sem_local.at[1])
+    load_d.start()
 
     barrier = pltpu.get_barrier_semaphore()
 
@@ -124,34 +137,69 @@
 
     greet(2 * z + 1 - core, y, x)
     greet(2 * mate + core, y, x)
-    count = 2
+    for step in range(1, 4):
+        greet(c, lax.rem(y + step, 4), x)
+    count = 5
     for t in range(4):
         to_c = 2 * dest(t) + core
         from_c = 2 * source_of(z, t) + core
-        if t:
-            greet(to_c, y, x)
-            greet(from_c, y, x)
-            count += 2
         for g in range(4):
             if t:
+                greet(to_c, y, g)
+                greet(from_c, y, g)
                 greet(to_c, g, y)
                 greet(from_c, x, g)
+                count += 4
             else:
+
+                @pl.when(x != g)
+                def _():
+                    greet(to_c, y, g)
 
                 @pl.when(jnp.logical_not((y == g) & diag))
                 def _():
                     greet(to_c, g, y)
                     greet(from_c, x, g)
 
-            count += 2
-
+    count = count + 3 + jnp.where(diag, 6, 8)
+
+    for req in range(8):
+        rlb[req] = jnp.full((1, 128), rl_ref[req, 0], jnp.int32)
+    load_d.wait()
+    for j in range(2):
+        dsend[:, j] = dkv[pl.ds(j, 64, stride=2), :].reshape(8, 8, 128)
     load.wait()
     for i in range(2):
         for s in range(2):
             for j in range(2):
                 sendb[2 * i + j, s] = raw[i, s, pl.ds(j, BLK, stride=2), :]
 
-    pl.semaphore_wait(barrier, jnp.where(diag, count - 2, count))
+    pl.semaphore_wait(barrier, count)
+
+    def y_copies(g):
+        reqs = pl.ds(2 * g, 2)
+        return [
+            pltpu.make_async_remote_copy(
+                src,
+                dst,
+                sem_y_s.at[g, n],
+                sem_y_r.at[y, n],
+                device_id=(c, g, x),
+                device_id_type=MESH,
+            )
+            for n, (src, dst) in enumerate(
+                ((dq_ref.at[reqs], rq.at[y]), (dsend.at[reqs], rd.at[y]), (rlb.at[reqs], rr.at[y]))
+            )
+        ]
+
+    def y_keep():
+        reqs = pl.ds(pl.multiple_of(2 * y, 2), 2)
+        return [
+            pltpu.make_async_copy(src, dst, sem_y_r.at[y, n])
+            for n, (src, dst) in enumerate(
+                ((dq_ref.at[reqs], rq.at[y]), (dsend.at[reqs], rd.at[y]), (rlb.at[reqs], rr.at[y]))
+            )
+        ]
 
     def pq_copy(t):
         zt = dest(t)
@@ -164,109 +212,143 @@
             src, dst, sem_pq_s.at[t], sem_pq_r.at[t], device_id=(2 * zt + core, y, x), device_id_type=MESH
         )
 
-    def dq_parts(t, g):
+    def dq_parts(t, h):
         p = dest(t) // 2
-        req = 2 * g + p // 2
+        i, j = p // 2, p % 2
         slot = 4 * t + x
         return (
-            (dq_ref.at[req, :, pl.ds(pl.multiple_of(8 * (p % 2), 8), 8), :], qb.at[pl.ds(64 + 4 * slot, 4)]),
-            (dkv_ref.at[req], db.at[slot]),
-            (rl_ref.at[req], lb.at[slot]),
-        )
-
-    def dq_remote(t, g, n, part):
+            (rq.at[h, i, :, pl.ds(pl.multiple_of(8 * j, 8), 8), :], qb.at[pl.ds(64 + 4 * slot, 4)]),
+            (rd.at[h, i, j], db.at[slot]),
+            (rr.at[h, i], lb.at[slot]),
+        )
+
+    def dq_remote(t, h, n, part):
         return pltpu.make_async_remote_copy(
             part[0],
             part[1],
-            sem_dq_s.at[4 * t + g, n],
+            sem_dq_s.at[4 * t + h, n],
             sem_dq_r.at[4 * t + x, n],
-            device_id=(2 * dest(t) + core, g, y),
+            device_id=(2 * dest(t) + core, y, h),
             device_id_type=MESH,
         )
 
-    def dq_start(t, g):
-        for n, part in enumerate(dq_parts(t, g)):
+    def dq_start(t, h):
+        for n, part in enumerate(dq_parts(t, h)):
             if t:
-                dq_remote(t, g, n, part).start()
+                dq_remote(t, h, n, part).start()
             else:
-                mine = (y == g) & diag
-
-                @pl.when(mine)
+
+                @pl.when(x == h)
                 def _():
                     pltpu.make_async_copy(part[0], part[1], sem_dq_r.at[4 * t + x, n]).start()
 
-                @pl.when(jnp.logical_not(mine))
+                @pl.when(x != h)
                 def _():
-                    dq_remote(t, g, n, part).start()
-
-    def dq_wait_send(t, g):
-        for n, part in enumerate(dq_parts(t, g)):
+                    dq_remote(t, h, n, part).start()
+
+    def dq_wait_send(t, h):
+        for n, part in enumerate(dq_parts(t, h)):
             if t:
-                dq_remote(t, g, n, part).wait_send()
+                dq_remote(t, h, n, part).wait_send()
             else:
 
-                @pl.when(jnp.logical_not((y == g) & diag))
+                @pl.when(x != h)
                 def _():
-                    dq_remote(t, g, n, part).wait_send()
-
-    def kv_primary(t):
+                    dq_remote(t, h, n, part).wait_send()
+
+    def piece(h):
+        return pl.ds(PIECE * h, PIECE)
+
+    def kv_primary(t, h):
         zt = dest(t)
         return pltpu.make_async_remote_copy(
-            sendb.at[zt // 2],
-            kvb.at[t],
-            sem_kp_s.at[t],
-            sem_k_r.at[t],
+            sendb.at[zt // 2, :, piece(h)],
+            kvb.at[t, :, piece(h)],
+            sem_kp_s.at[t, h],
+            sem_k_r.at[t, h],
             device_id=(2 * zt + core, y, x),
             device_id_type=MESH,
         )
 
-    def kv_forward(t):
-        return pltpu.make_async_remote_copy(
-            kvb.at[t],
-            kvb.at[t + 4],
-            sem_kf_s.at[t],
-            sem_k_r.at[t + 4],
+    def kv_forward(t, h):
+        return pltpu.make_async_remote_copy(
+            kvb.at[t, :, piece(h)],
+            kvb.at[t + 4, :, piece(h)],
+            sem_kf_s.at[t, h],
+            sem_k_r.at[t + 4, h],
             device_id=(2 * mate + core, y, x),
             device_id_type=MESH,
         )
 
-    def kv_cross(u):
-        return pltpu.make_async_remote_copy(
-            kvb.at[u],
-            kvb.at[u + 8],
-            sem_kx_s.at[u],
-            sem_k_r.at[u + 8],
+    def kv_cross(u, h):
+        return pltpu.make_async_remote_copy(
+            kvb.at[u, :, piece(h)],
+            kvb.at[u + 8, :, piece(h)],
+            sem_kx_s.at[u, h],
+            sem_k_r.at[u + 8, h],
             device_id=(2 * z + 1 - core, y, x),
             device_id_type=MESH,
         )
 
-    keep = pltpu.make_async_copy(sendb.at[pair], kvb.at[0], sem_k_r.at[0])
-    keep.start()
+    def arrive(u):
+        for h in range(PIECES):
+            part = kvb.at[u, :, piece(h)]
+            pltpu.make_async_copy(part, part, sem_k_r.at[u, h]).wait()
+
+            @pl.when(u < 4)
+            def _():
+                kv_forward(u, h).start()
+
+            kv_cross(u, h).start()
+
+    def crossed(u):
+        for h in range(PIECES):
+            part = kvb.at[u, :, piece(h)]
+            pltpu.make_async_copy(part, part, sem_k_r.at[u, h]).wait()
+
+    for h in range(PIECES):
+        pltpu.make_async_copy(sendb.at[pair, :, piece(h)], kvb.at[0, :, piece(h)], sem_k_r.at[0, h]).start()
+    for g in range(4):
+
+        @pl.when(y == g)
+        def _():
+            for copy in y_keep():
+                copy.start()
+
+        @pl.when(y != g)
+        def _():
+            for copy in y_copies(g):
+                copy.start()
+
     for t in (3, 2, 1, 0):
         pq_copy(t).start()
-        for g in range(4):
+    for t in (2, 1):
+        for h in range(PIECES):
+            kv_primary(t, h).start()
+
+    arrive(jnp.int32(0))
+
+    for g in range(4):
+        for n, part in enumerate((rq.at[g], rd.at[g], rr.at[g])):
+            pltpu.make_async_copy(part, part, sem_y_r.at[g, n]).wait()
+        for t in (3, 2, 1, 0):
             dq_start(t, g)
-    for t in (3, 2, 1):
-        kv_primary(t).start()
-
-    def arrive(u):
-        pltpu.make_async_copy(kvb.at[u], kvb.at[u], sem_k_r.at[u]).wait()
-
-        @pl.when(u < 4)
-        def _():
-            kv_forward(u).start()
-
-        @pl.when(u < 8)
-        def _():
-            kv_cross(u).start()
-
-    arrive(jnp.int32(0))
+    for h in range(PIECES):
+        kv_primary(3, h).start()
+
 
     own_len = len_ref[2 * y + own_i]
     lane = lax.broadcasted_iota(jnp.int32, (1, 128), 1)
     for t in range(4):
         first = own_len - (span - 1) + 16 * (2 * source_of(z, t) + core)
         lim[:, pl.ds(128 * t, 128)] = first + lane // 8
+
+    def own_slot(m):
+        return jnp.where(m == 2, 4, jnp.where(m == 3, 2, jnp.where(m == 4, 3, m)))
+
+    for m in range(1, AHEAD):
+        arrive(own_slot(jnp.int32(m)))
+
 
     for t in range(4):
         part = qb.at[pl.ds(16 * t, 16)]
@@ -295,10 +377,8 @@
     m_ref[:, :HALF] = jnp.full((1, HALF), NEG_FILL, F32)
     l_ref[:, :HALF] = jnp.zeros((1, HALF), F32)
     acc[:, :HALF] = jnp.zeros((128, HALF), F32)
-    drafts = db[...].reshape(64, 4, 128)
-    dk = jnp.where(own_j == 0, drafts[:, 0], drafts[:, 1])
-    dv = jnp.where(own_j == 0, drafts[:, 2], drafts[:, 3])
-    s = dot_nt(key_terms(dk), q6[pl.ds(HALF, HALF), :])
+    drafts = db[...].reshape(64, 2, 128)
+    s = dot_nt(key_terms(drafts[:, 0]), q6[pl.ds(HALF, HALF), :])
     key_id = lax.broadcasted_iota(jnp.int32, (64, HALF), 0)
     query_id = lax.broadcasted_iota(jnp.int32, (64, HALF), 1) // 8
     s = jnp.where((key_id // 4 == query_id // 4) & (key_id <= query_id), s, NEG_FILL)
@@ -306,29 +386,26 @@
     p = jnp.exp2(s - top)
     m_ref[:, HALF:] = top
     l_ref[:, HALF:] = jnp.sum(p, axis=0, keepdims=True)
-    acc[:, HALF:] = weighted(value_terms(dv), p)
-
-    def order(n):
-        return n // 4 + (n % 2) * 8 + ((n // 2) % 2) * 4
-
-    @pl.loop(0, 16)
-    def _(n):
-        u = order(n)
-
-        @pl.when(n < 15)
+    acc[:, HALF:] = weighted(value_terms(drafts[:, 1]), p)
+
+    @pl.loop(0, 8)
+    def _(m):
+        u = own_slot(m)
+
+        @pl.when(m + AHEAD < 8)
         def _():
-            arrive(order(n + 1))
-
-        t = u % 4
-        chip = jnp.where((u // 4) % 2 == 0, z, mate)
-        owner = jnp.where(u < 8, core, 1 - core)
-        first = BLK * (2 * source_of(chip, t) + owner)
-        k6[...] = key_terms(kvb[u, 0])
-        v2b[...] = value_terms(kvb[u, 1])
+            arrive(own_slot(m + AHEAD))
+
+        crossed(u + 8)
+        first = 2 * BLK * source_of(jnp.where(u < 4, z, mate), u % 4)
+        for k in range(2):
+            owner = core if k == 0 else 1 - core
+            k6[owner] = key_terms(kvb[u + 8 * k, 0])
+            v2b[owner] = value_terms(kvb[u + 8 * k, 1])
         for qc in range(NQ // QC):
             cols = pl.ds(QC * qc, QC)
-            s = dot_nt(k6[...], q6[pl.ds(QC * qc, QC), :])
-            place = lax.broadcasted_iota(jnp.int32, (BLK, QC), 0)
+            s = dot_nt(k6[...].reshape(2 * BLK, 768), q6[pl.ds(QC * qc, QC), :])
+            place = lax.broadcasted_iota(jnp.int32, (2 * BLK, QC), 0)
             s = jnp.where(place < lim[:, cols] - first, s, NEG_FILL)
             old = m_ref[:, cols]
             top = jnp.maximum(old, jnp.max(s, axis=0, keepdims=True))
@@ -336,7 +413,8 @@
             p = jnp.exp2(s - top)
             m_ref[:, cols] = top
             l_ref[:, cols] = l_ref[:, cols] * fade + jnp.sum(p, axis=0, keepdims=True)
-            acc[:, cols] = acc[:, cols] * fade + weighted(v2b[...], p)
+            values = jnp.concatenate([v2b[0], v2b[1]], axis=1)
+            acc[:, cols] = acc[:, cols] * fade + weighted(values, p)
 
     rows_j = pl.ds(pl.multiple_of(8 * own_j, 8), 8)
 
@@ -384,7 +462,7 @@
             do_remote(t, r).start()
 
     for qc in (3, 1, 2, 0):
-        cols = pl.ds(QC * qc, QC)
+        cols = pl.ds(256 * qc, 256)
         out = acc[:, cols] * (1.0 / l_ref[:, cols])
         ob[pl.ds(32 * qc, 32)] = out.T.reshape(32, 8, 128)
         for t in (2 * (qc % 2) + 1, 2 * (qc % 2)):
@@ -394,15 +472,25 @@
                 for r in range(4):
                     do_start(t, r)
 
+    for g in range(4):
+
+        @pl.when(y != g)
+        def _():
+            for copy in y_copies(g):
+                copy.wait_send()
+
     for t in range(1, 4):
         pq_copy(t).wait_send()
-        kv_primary(t).wait_send()
     for t in range(4):
         for g in range(4):
             dq_wait_send(t, g)
-        kv_forward(t).wait_send()
+        for h in range(PIECES):
+            if t:
+                kv_primary(t, h).wait_send()
+            kv_forward(t, h).wait_send()
     for u in range(8):
-        kv_cross(u).wait_send()
+        for h in range(PIECES):
+            kv_cross(u, h).wait_send()
     for t in range(4):
         if t:
             po_copy(t).wait_send()
@@ -427,7 +515,6 @@
     head_dim = prefill_q.shape[-1]
     span = prefill_q.shape[1] * lax.axis_size("ctx")
     scale = math.log2(math.e) / math.sqrt(head_dim)
-    limits = jnp.broadcast_to(row_length[:, :, None], (8, 1, 128))
     hbm = pl.BlockSpec(memory_space=pltpu.MemorySpace.HBM)
     dma = pltpu.SemaphoreType.DMA
     prefill_out, decode_out = pl.pallas_call(
@@ -436,32 +523,40 @@
             jax.ShapeDtypeStruct((2, 16, 16, 128), F32),
             jax.ShapeDtypeStruct((8, 4, 16, 128), F32),
         ),
-        in_specs=[pl.BlockSpec(memory_space=pltpu.SMEM)] + [hbm] * 5,
+        in_specs=[pl.BlockSpec(memory_space=pltpu.SMEM)] * 2 + [hbm] * 4,
         out_specs=(hbm, hbm),
         scratch_shapes=[
             pltpu.VMEM((2, 2, 512, 128), F32),
             pltpu.VMEM((4, 2, BLK, 128), F32),
             pltpu.VMEM((16, 2, BLK, 128), F32),
+            pltpu.VMEM((128, 128), F32),
+            pltpu.VMEM((8, 2, 8, 128), F32),
+            pltpu.VMEM((8, 1, 128), jnp.int32),
+            pltpu.VMEM((4, 2, 4, 16, 128), F32),
+            pltpu.VMEM((4, 2, 2, 8, 128), F32),
+            pltpu.VMEM((4, 2, 1, 128), jnp.int32),
             pltpu.VMEM((128, 8, 128), F32),
             pltpu.VMEM((16, 1, 128), jnp.int32),
-            pltpu.VMEM((16, 16, 128), F32),
+            pltpu.VMEM((16, 8, 128), F32),
             pltpu.VMEM((NQ, 768), BF16),
-            pltpu.VMEM((BLK, 768), BF16),
-            pltpu.VMEM((256, BLK), BF16),
+            pltpu.VMEM((2, BLK, 768), BF16),
+            pltpu.VMEM((2, 256, BLK), BF16),
             pltpu.VMEM((1, NQ), jnp.int32),
             pltpu.VMEM((1, NQ), F32),
             pltpu.VMEM((1, NQ), F32),
             pltpu.VMEM((128, NQ), F32),
             pltpu.VMEM((128, 8, 128), F32),
-            dma((1,)),
+            dma((2,)),
+            dma((4, 3)),
+            dma((4, 3)),
             dma((4,)),
             dma((4,)),
             dma((16, 3)),
             dma((16, 3)),
-            dma((4,)),
-            dma((4,)),
-            dma((8,)),
-            dma((16,)),
+            dma((4, PIECES)),
+            dma((4, PIECES)),
+            dma((8, PIECES)),
+            dma((16, PIECES)),
             dma((4,)),
             dma((4,)),
             dma((16,)),
@@ -472,11 +567,11 @@
         ),
     )(
         lengths,
-        limits,
+        row_length,
         kv_cache.reshape(2, 2, 512, 128),
         prefill_q,
         decode_q.reshape(8, 4, 16, 128),
-        decode_kv.reshape(8, 16, 128),
+        decode_kv.reshape(128, 128),
     )
     return prefill_out, decode_out.reshape(decode_q.shape)
 

time: 105 us -> 84.9 us (0.81)
  Pallas kernels: 100 us -> 80.3 us
    pallas_call x1, Pallas kernels: 100 us -> 80.3 us  [on_device(): pl.pallas_call(functools.partial(kernel, scale, span), out_shape=(jax.Sha...]
    unnamed x6 -> x7, local copies, waits for them, and re-layouts: 3.07 us -> 3.74 us
where the time goes in v1:
time: 84.9 us; the launch traced here: 84.7 us
  Pallas kernels  80.3 us (95%)
  local copies, waits for them, and re-layouts  3.74 us (4%)
    pallas_call x1, Pallas kernels, on_device(): pl.pallas_call(functools.partial(kernel, scale, span), out_shape=(jax.Sha...  80.3 us
    unnamed x7, local copies, waits for them, and re-layouts  3.74 us

profile of v1, /device:TPU:24, one launch (start us, length us, event | category | flops | bytes accessed | tf_op | source)
XLA Modules:
  0.0 84.7 jit_solution(17016967948804206302)
XLA Ops:
  0.6 0.0 copy-start.1
  0.6 0.6 copy-done.1
  1.3 0.7 copy.8.rl_ref
  2.0 80.3 %shard_map.77 = (f32[2,16,16,128]{3,2,1,0:T(8,128)}, f32[8,4,16,128]{3,2,1,0:T(8,128)}) custom-call(s32[8]{0:T(128)} %len_ref.1, s32[8,1]{1,0:T(8,128)} %copy.8.rl_ref, f32[2,2,512,128]{3,2,1,0:T(8,128)} %bitcast.6, f32[2,16,16,128]{3,2,1,0:T(8,128)} %pq_ref.1, f32[8,4,16,128]{3,2,1,0:T(8,128)} %bitcast.8, f32[128,128]{1,0:T(8,128)} %bitcast.9), custom_call_target="tpu_custom_call" | custom-call | tf_op jit(solution)/shard_map/pallas_call | solution.py:520
  82.3 0.0 copy-start
  82.3 1.7 %copy.12 = f32[2,16,16,128]{3,2,1,0:T(8,128)} copy(f32[2,16,16,128]{3,2,1,0:T(8,128)} %get-tuple-element.10) | data formatting | bytes 524288
  84.0 0.0 copy-done
  84.0 0.7 copy.13
Async XLA Ops:
  0.6 0.7 copy-start.1
  82.3 1.7 %copy-start = (f32[8,4,16,128]{3,2,1,0:T(8,128)S(1)}, f32[8,4,16,128]{3,2,1,0:T(8,128)}, u32[]{:S(2)}) copy-start(f32[8,4,16,128]{3,2,1,0:T(8,128)} %get-tuple-element.5) | copy-start | bytes 786436

commit v2 on v1

--- a/solution.py
+++ b/solution.py
@@ -19,7 +19,36 @@
 QC = 512
 PIECES = 2
 PIECE = BLK // PIECES
+OWN = (0, 1, 4, 2, 3, 5, 6, 7)
 AHEAD = 1
+PLAN = (
+    ("y", 0),
+    ("keep", 0),
+    ("prefill", 1),
+    ("prefill", 0),
+    ("hear", 0),
+    ("tell", 1),
+    ("prefill", 2),
+    ("hear", 1),
+    ("tell", 2),
+    ("prefill", 3),
+    ("relay", 0),
+    ("decode", 1),
+    ("hear", 2),
+    ("decode", 3),
+    ("decode", 2),
+    ("decode", 0),
+    ("keys", (1, 0)),
+    ("arrive", (0, 0)),
+    ("keys", (1, 1)),
+    ("arrive", (0, 1)),
+    ("keys", (2, 0)),
+    ("keys", (2, 1)),
+    ("keys", (3, 0)),
+    ("keys", (3, 1)),
+    ("arrive", (1, 0)),
+)
+LAST = max(PIECES * which[0] + which[1] for what, which in PLAN if what == "arrive")
 
 
 def split2(x):
@@ -91,6 +120,7 @@
     acc,
     ob,
     sem_local,
+    near,
     sem_y_s,
     sem_y_r,
     sem_pq_s,
@@ -135,36 +165,17 @@
     def greet(ctx, head, rep):
         pl.semaphore_signal(barrier, inc=1, device_id=(ctx, head, rep), device_id_type=MESH)
 
+    up = 2 * lax.rem(z + 1, CHIPS) + core
+    down = 2 * lax.rem(z + CHIPS - 1, CHIPS) + core
     greet(2 * z + 1 - core, y, x)
-    greet(2 * mate + core, y, x)
+    greet(up, y, x)
+    greet(down, y, x)
     for step in range(1, 4):
         greet(c, lax.rem(y + step, 4), x)
-    count = 5
-    for t in range(4):
-        to_c = 2 * dest(t) + core
-        from_c = 2 * source_of(z, t) + core
-        for g in range(4):
-            if t:
-                greet(to_c, y, g)
-                greet(from_c, y, g)
-                greet(to_c, g, y)
-                greet(from_c, x, g)
-                count += 4
-            else:
-
-                @pl.when(x != g)
-                def _():
-                    greet(to_c, y, g)
-
-                @pl.when(jnp.logical_not((y == g) & diag))
-                def _():
-                    greet(to_c, g, y)
-                    greet(from_c, x, g)
-
-    count = count + 3 + jnp.where(diag, 6, 8)
+        greet(c, y, lax.rem(x + step, 4))
 
     for req in range(8):
-        rlb[req] = jnp.full((1, 128), rl_ref[req, 0], jnp.int32)
+        rlb[req] = jnp.full((1, 128), rl_ref[req], jnp.int32)
     load_d.wait()
     for j in range(2):
         dsend[:, j] = dkv[pl.ds(j, 64, stride=2), :].reshape(8, 8, 128)
@@ -174,7 +185,16 @@
             for j in range(2):
                 sendb[2 * i + j, s] = raw[i, s, pl.ds(j, BLK, stride=2), :]
 
-    pl.semaphore_wait(barrier, count)
+    pl.semaphore_wait(barrier, 9)
+
+    def tell(n):
+        for there in (up, down):
+            pl.semaphore_signal(near.at[n], inc=1, device_id=(there, y, x), device_id_type=MESH)
+
+    def hear(n):
+        pl.semaphore_wait(near.at[n], 2)
+
+    tell(0)
 
     def y_copies(g):
         reqs = pl.ds(2 * g, 2)
@@ -290,65 +310,73 @@
             device_id_type=MESH,
         )
 
-    def arrive(u):
-        for h in range(PIECES):
-            part = kvb.at[u, :, piece(h)]
-            pltpu.make_async_copy(part, part, sem_k_r.at[u, h]).wait()
-
-            @pl.when(u < 4)
-            def _():
-                kv_forward(u, h).start()
-
-            kv_cross(u, h).start()
+    def arrive(u, h):
+        part = kvb.at[u, :, piece(h)]
+        pltpu.make_async_copy(part, part, sem_k_r.at[u, h]).wait()
+
+        @pl.when(u < 4)
+        def _():
+            kv_forward(u, h).start()
+
+        kv_cross(u, h).start()
 
     def crossed(u):
         for h in range(PIECES):
             part = kvb.at[u, :, piece(h)]
             pltpu.make_async_copy(part, part, sem_k_r.at[u, h]).wait()
 
-    for h in range(PIECES):
-        pltpu.make_async_copy(sendb.at[pair, :, piece(h)], kvb.at[0, :, piece(h)], sem_k_r.at[0, h]).start()
-    for g in range(4):
-
-        @pl.when(y == g)
-        def _():
-            for copy in y_keep():
-                copy.start()
-
-        @pl.when(y != g)
-        def _():
-            for copy in y_copies(g):
-                copy.start()
-
-    for t in (3, 2, 1, 0):
-        pq_copy(t).start()
-    for t in (2, 1):
-        for h in range(PIECES):
-            kv_primary(t, h).start()
-
-    arrive(jnp.int32(0))
-
-    for g in range(4):
-        for n, part in enumerate((rq.at[g], rd.at[g], rr.at[g])):
-            pltpu.make_async_copy(part, part, sem_y_r.at[g, n]).wait()
-        for t in (3, 2, 1, 0):
-            dq_start(t, g)
-    for h in range(PIECES):
-        kv_primary(3, h).start()
-
+    def along_y():
+        for g in range(4):
+
+            @pl.when(y == g)
+            def _():
+                for copy in y_keep():
+                    copy.start()
+
+            @pl.when(y != g)
+            def _():
+                for copy in y_copies(g):
+                    copy.start()
+
+    def along_y_done():
+        for g in range(4):
+            for n, part in enumerate((rq.at[g], rd.at[g], rr.at[g])):
+                pltpu.make_async_copy(part, part, sem_y_r.at[g, n]).wait()
+
+    def own_slot(m):
+        slot = OWN[-1]
+        for place, value in enumerate(OWN[:-1]):
+            slot = jnp.where(m == place, value, slot)
+        return slot
+
+    for what, which in PLAN:
+        if what == "hear":
+            hear(which)
+        elif what == "tell":
+            tell(which)
+        elif what == "y":
+            along_y()
+        elif what == "relay":
+            along_y_done()
+        elif what == "prefill":
+            pq_copy(which).start()
+        elif what == "decode":
+            for g in range(4):
+                dq_start(which, g)
+        elif what == "keys":
+            kv_primary(*which).start()
+        elif what == "keep":
+            for h in range(PIECES):
+                src, dst = sendb.at[pair, :, piece(h)], kvb.at[0, :, piece(h)]
+                pltpu.make_async_copy(src, dst, sem_k_r.at[0, h]).start()
+        elif what == "arrive":
+            arrive(jnp.int32(OWN[which[0]]), which[1])
 
     own_len = len_ref[2 * y + own_i]
     lane = lax.broadcasted_iota(jnp.int32, (1, 128), 1)
     for t in range(4):
         first = own_len - (span - 1) + 16 * (2 * source_of(z, t) + core)
         lim[:, pl.ds(128 * t, 128)] = first + lane // 8
-
-    def own_slot(m):
-        return jnp.where(m == 2, 4, jnp.where(m == 3, 2, jnp.where(m == 4, 3, m)))
-
-    for m in range(1, AHEAD):
-        arrive(own_slot(jnp.int32(m)))
-
 
     for t in range(4):
         part = qb.at[pl.ds(16 * t, 16)]
@@ -392,9 +420,11 @@
     def _(m):
         u = own_slot(m)
 
-        @pl.when(m + AHEAD < 8)
-        def _():
-            arrive(own_slot(m + AHEAD))
+        for h in range(PIECES):
+
+            @pl.when((m + AHEAD < 8) & (PIECES * (m + AHEAD) + h > LAST))
+            def _():
+                arrive(own_slot(m + AHEAD), h)
 
         crossed(u + 8)
         first = 2 * BLK * source_of(jnp.where(u < 4, z, mate), u % 4)
@@ -547,6 +577,7 @@
             pltpu.VMEM((128, NQ), F32),
             pltpu.VMEM((128, 8, 128), F32),
             dma((2,)),
+            pltpu.SemaphoreType.REGULAR((3,)),
             dma((4, 3)),
             dma((4, 3)),
             dma((4,)),
@@ -567,7 +598,7 @@
         ),
     )(
         lengths,
-        row_length,
+        row_length.reshape(8),
         kv_cache.reshape(2, 2, 512, 128),
         prefill_q,
         decode_q.reshape(8, 4, 16, 128),

time: 84.9 us -> 80.7 us (0.951); the launches traced: 84.7 us -> 79.2 us
  Pallas kernels: 80.3 us -> 76.1 us
  local copies, waits for them, and re-layouts: 3.74 us -> 2.42 us
    pallas_call x1, Pallas kernels: 80.3 us -> 76.1 us  [on_device(): pl.pallas_call(functools.partial(kernel, scale, span), out_shape=(jax.Sha...]
    unnamed x7 -> x4, local copies, waits for them, and re-layouts: 3.74 us -> 2.42 us
where the time goes in v2:
time: 80.7 us; the launch traced here: 79.2 us
  Pallas kernels  76.1 us (94%)
  local copies, waits for them, and re-layouts  2.42 us (3%)
    pallas_call x1, Pallas kernels, on_device(): pl.pallas_call(functools.partial(kernel, scale, span), out_shape=(jax.Sha...  76.1 us
    unnamed x4, local copies, waits for them, and re-layouts  2.42 us

profile of v2, /device:TPU:24, one launch (start us, length us, event | category | flops | bytes accessed | tf_op | source)
XLA Modules:
  0.0 79.2 jit_solution(16171156773841494259)
XLA Ops:
  0.6 76.1 %shard_map.77 = (f32[2,16,16,128]{3,2,1,0:T(8,128)}, f32[8,4,16,128]{3,2,1,0:T(8,128)}) custom-call(s32[8]{0:T(128)} %len_ref.1, s32[8]{0:T(128)} %bitcast.11, f32[2,2,512,128]{3,2,1,0:T(8,128)} %bitcast.7, f32[2,16,16,128]{3,2,1,0:T(8,128)} %pq_ref.1, f32[8,4,16,128]{3,2,1,0:T(8,128)} %bitcast.9, f32[128,128]{1,0:T(8,128)} %bitcast.10), custom_call_target="tpu_custom_call" | custom-call | tf_op jit(solution)/shard_map/pallas_call | solution.py:550
  76.7 0.0 copy-start
  76.7 1.7 %copy.11 = f32[2,16,16,128]{3,2,1,0:T(8,128)} copy(f32[2,16,16,128]{3,2,1,0:T(8,128)} %get-tuple-element.10) | data formatting | bytes 524288
  78.5 0.0 copy-done
  78.5 0.7 copy.12
Async XLA Ops:
  76.7 1.7 %copy-start = (f32[8,4,16,128]{3,2,1,0:T(8,128)S(1)}, f32[8,4,16,128]{3,2,1,0:T(8,128)}, u32[]{:S(2)}) copy-start(f32[8,4,16,128]{3,2,1,0:T(8,128)} %get-tuple-element.5) | copy-start | bytes 786436

commit v3 on v2

--- a/solution.py
+++ b/solution.py
@@ -13,42 +13,58 @@
 F32 = jnp.float32
 BF16 = jnp.bfloat16
 CHIPS = 8
-NQ = 1024
 HALF = 512
 BLK = 256
-QC = 512
 PIECES = 2
 PIECE = BLK // PIECES
-OWN = (0, 1, 4, 2, 3, 5, 6, 7)
-AHEAD = 1
+OWN = (0, 4, 1, 5, 3, 2, 7, 6)
+SPOT = (1, 1)
 PLAN = (
     ("y", 0),
     ("keep", 0),
     ("prefill", 1),
     ("prefill", 0),
+    ("arrive", (0, 0)),
     ("hear", 0),
     ("tell", 1),
     ("prefill", 2),
+    ("arrive", (0, 1)),
     ("hear", 1),
     ("tell", 2),
     ("prefill", 3),
+    ("keys", (1, 0)),
+    ("keys", (1, 1)),
+    ("keys", (2, 0)),
     ("relay", 0),
-    ("decode", 1),
     ("hear", 2),
     ("decode", 3),
+    ("decode", 1),
     ("decode", 2),
     ("decode", 0),
-    ("keys", (1, 0)),
-    ("arrive", (0, 0)),
-    ("keys", (1, 1)),
-    ("arrive", (0, 1)),
-    ("keys", (2, 0)),
+    ("keys", (3, 0)),
     ("keys", (2, 1)),
-    ("keys", (3, 0)),
     ("keys", (3, 1)),
+    ("prefill queries", 0),
+    ("ready", 0),
+    ("attend", (0, 0)),
     ("arrive", (1, 0)),
+    ("arrive", (1, 1)),
+    ("ready", 1),
+    ("attend", (1, 0)),
+    ("arrive", (2, 0)),
+    ("arrive", (2, 1)),
+    ("ready", 2),
+    ("attend", (2, 0)),
+    ("arrive", (5, 0)),
+    ("decode queries", 0),
+    ("attend", (0, 1)),
+    ("attend", (1, 1)),
+    ("arrive", (3, 0)),
+    ("arrive", (3, 1)),
+    ("attend", (2, 1)),
+    ("arrive", (4, 0)),
 )
-LAST = max(PIECES * which[0] + which[1] for what, which in PLAN if what == "arrive")
+EARLY = 1 + max(which for what, which in PLAN if what == "ready")
 
 
 def split2(x):
@@ -349,6 +365,77 @@
             slot = jnp.where(m == place, value, slot)
         return slot
 
+    own_len = len_ref[2 * y + own_i]
+    lane = lax.broadcasted_iota(jnp.int32, (1, 128), 1)
+    for t in range(4):
+        first = own_len - (span - 1) + 16 * (2 * source_of(z, t) + core)
+        lim[0, :, pl.ds(128 * t, 128)] = first + lane // 8
+
+    def split_queries(part):
+        @pl.loop(0, HALF // 128)
+        def _(n):
+            q = qb[pl.ds(64 * part + 16 * n, 16)].reshape(128, 128) * scale
+            q6[part, pl.ds(pl.multiple_of(128 * n, 128), 128), :] = query_terms(q)
+
+    def prefill_queries():
+        for t in range(4):
+            part = qb.at[pl.ds(16 * t, 16)]
+            pltpu.make_async_copy(part, part, sem_pq_r.at[t]).wait()
+        split_queries(0)
+        m_ref[0] = jnp.full((1, HALF), NEG_FILL, F32)
+        l_ref[0] = jnp.zeros((1, HALF), F32)
+        acc[0] = jnp.zeros((128, HALF), F32)
+
+    def decode_queries():
+        @pl.loop(0, 16)
+        def _(s):
+            part = qb.at[pl.ds(64 + 4 * s, 4)]
+            pltpu.make_async_copy(part, part, sem_dq_r.at[s, 0]).wait()
+            pltpu.make_async_copy(db.at[s], db.at[s], sem_dq_r.at[s, 1]).wait()
+            pltpu.make_async_copy(lb.at[s], lb.at[s], sem_dq_r.at[s, 2]).wait()
+
+        for v in range(4):
+            row = jnp.where(
+                lane < 64,
+                jnp.where(lane < 32, lb[4 * v], lb[4 * v + 1]),
+                jnp.where(lane < 96, lb[4 * v + 2], lb[4 * v + 3]),
+            )
+            lim[1, :, pl.ds(128 * v, 128)] = row
+        split_queries(1)
+        drafts = db[...].reshape(64, 2, 128)
+        s = dot_nt(key_terms(drafts[:, 0]), q6[1])
+        key_id = lax.broadcasted_iota(jnp.int32, (64, HALF), 0)
+        query_id = lax.broadcasted_iota(jnp.int32, (64, HALF), 1) // 8
+        s = jnp.where((key_id // 4 == query_id // 4) & (key_id <= query_id), s, NEG_FILL)
+        top = jnp.max(s, axis=0, keepdims=True)
+        p = jnp.exp2(s - top)
+        m_ref[1] = top
+        l_ref[1] = jnp.sum(p, axis=0, keepdims=True)
+        acc[1] = weighted(value_terms(drafts[:, 1]), p)
+
+    def ready(m):
+        u = own_slot(m)
+        crossed(u + 8)
+        for k in range(2):
+            owner = core if k == 0 else 1 - core
+            k6[m, owner] = key_terms(kvb[u + 8 * k, 0])
+            v2b[m, owner] = value_terms(kvb[u + 8 * k, 1])
+
+    def attend(m, part):
+        u = own_slot(m)
+        first = 2 * BLK * source_of(jnp.where(u < 4, z, mate), u % 4)
+        s = dot_nt(k6[m].reshape(2 * BLK, 768), q6[part])
+        place = lax.broadcasted_iota(jnp.int32, (2 * BLK, HALF), 0)
+        s = jnp.where(place < lim[part] - first, s, NEG_FILL)
+        old = m_ref[part]
+        top = jnp.maximum(old, jnp.max(s, axis=0, keepdims=True))
+        fade = jnp.exp2(old - top)
+        p = jnp.exp2(s - top)
+        m_ref[part] = top
+        l_ref[part] = l_ref[part] * fade + jnp.sum(p, axis=0, keepdims=True)
+        values = jnp.concatenate([v2b[m, 0], v2b[m, 1]], axis=1)
+        acc[part] = acc[part] * fade + weighted(values, p)
+
     for what, which in PLAN:
         if what == "hear":
             hear(which)
@@ -371,80 +458,36 @@
                 pltpu.make_async_copy(src, dst, sem_k_r.at[0, h]).start()
         elif what == "arrive":
             arrive(jnp.int32(OWN[which[0]]), which[1])
-
-    own_len = len_ref[2 * y + own_i]
-    lane = lax.broadcasted_iota(jnp.int32, (1, 128), 1)
-    for t in range(4):
-        first = own_len - (span - 1) + 16 * (2 * source_of(z, t) + core)
-        lim[:, pl.ds(128 * t, 128)] = first + lane // 8
-
-    for t in range(4):
-        part = qb.at[pl.ds(16 * t, 16)]
-        pltpu.make_async_copy(part, part, sem_pq_r.at[t]).wait()
-
-    @pl.loop(0, 16)
-    def _(s):
-        part = qb.at[pl.ds(64 + 4 * s, 4)]
-        pltpu.make_async_copy(part, part, sem_dq_r.at[s, 0]).wait()
-        pltpu.make_async_copy(db.at[s], db.at[s], sem_dq_r.at[s, 1]).wait()
-        pltpu.make_async_copy(lb.at[s], lb.at[s], sem_dq_r.at[s, 2]).wait()
-
-    for v in range(4):
-        row = jnp.where(
-            lane < 64,
-            jnp.where(lane < 32, lb[4 * v], lb[4 * v + 1]),
-            jnp.where(lane < 96, lb[4 * v + 2], lb[4 * v + 3]),
-        )
-        lim[:, pl.ds(HALF + 128 * v, 128)] = row
-
-    @pl.loop(0, NQ // 128)
-    def _(n):
-        q = qb[pl.ds(16 * n, 16)].reshape(128, 128) * scale
-        q6[pl.ds(pl.multiple_of(128 * n, 128), 128), :] = query_terms(q)
-
-    m_ref[:, :HALF] = jnp.full((1, HALF), NEG_FILL, F32)
-    l_ref[:, :HALF] = jnp.zeros((1, HALF), F32)
-    acc[:, :HALF] = jnp.zeros((128, HALF), F32)
-    drafts = db[...].reshape(64, 2, 128)
-    s = dot_nt(key_terms(drafts[:, 0]), q6[pl.ds(HALF, HALF), :])
-    key_id = lax.broadcasted_iota(jnp.int32, (64, HALF), 0)
-    query_id = lax.broadcasted_iota(jnp.int32, (64, HALF), 1) // 8
-    s = jnp.where((key_id // 4 == query_id // 4) & (key_id <= query_id), s, NEG_FILL)
-    top = jnp.max(s, axis=0, keepdims=True)
-    p = jnp.exp2(s - top)
-    m_ref[:, HALF:] = top
-    l_ref[:, HALF:] = jnp.sum(p, axis=0, keepdims=True)
-    acc[:, HALF:] = weighted(value_terms(drafts[:, 1]), p)
-
-    @pl.loop(0, 8)
+        elif what == "prefill queries":
+            prefill_queries()
+        elif what == "decode queries":
+            decode_queries()
+        elif what == "ready":
+            ready(which)
+        elif what == "attend":
+            attend(*which)
+
+    def send_on(m, spot):
+        for h in range(PIECES):
+            if SPOT[h] != spot:
+                continue
+            go = m + 1 < 8
+            for name, place in PLAN:
+                if name == "arrive" and place[1] == h and place[0] > EARLY:
+                    go = go & (m + 1 != place[0])
+
+            @pl.when(go)
+            def _():
+                arrive(own_slot(m + 1), h)
+
+    @pl.loop(EARLY, 7)
     def _(m):
-        u = own_slot(m)
-
-        for h in range(PIECES):
-
-            @pl.when((m + AHEAD < 8) & (PIECES * (m + AHEAD) + h > LAST))
-            def _():
-                arrive(own_slot(m + AHEAD), h)
-
-        crossed(u + 8)
-        first = 2 * BLK * source_of(jnp.where(u < 4, z, mate), u % 4)
-        for k in range(2):
-            owner = core if k == 0 else 1 - core
-            k6[owner] = key_terms(kvb[u + 8 * k, 0])
-            v2b[owner] = value_terms(kvb[u + 8 * k, 1])
-        for qc in range(NQ // QC):
-            cols = pl.ds(QC * qc, QC)
-            s = dot_nt(k6[...].reshape(2 * BLK, 768), q6[pl.ds(QC * qc, QC), :])
-            place = lax.broadcasted_iota(jnp.int32, (2 * BLK, QC), 0)
-            s = jnp.where(place < lim[:, cols] - first, s, NEG_FILL)
-            old = m_ref[:, cols]
-            top = jnp.maximum(old, jnp.max(s, axis=0, keepdims=True))
-            fade = jnp.exp2(old - top)
-            p = jnp.exp2(s - top)
-            m_ref[:, cols] = top
-            l_ref[:, cols] = l_ref[:, cols] * fade + jnp.sum(p, axis=0, keepdims=True)
-            values = jnp.concatenate([v2b[0], v2b[1]], axis=1)
-            acc[:, cols] = acc[:, cols] * fade + weighted(values, p)
+        send_on(m, 0)
+        ready(m)
+        attend(m, 0)
+        send_on(m, 1)
+        attend(m, 1)
+        send_on(m, 2)
 
     rows_j = pl.ds(pl.multiple_of(8 * own_j, 8), 8)
 
@@ -491,9 +534,12 @@
         def _():
             do_remote(t, r).start()
 
-    for qc in (3, 1, 2, 0):
-        cols = pl.ds(256 * qc, 256)
-        out = acc[:, cols] * (1.0 / l_ref[:, cols])
+    ready(7)
+    for qc in (3, 2, 1, 0):
+        if qc % 2:
+            attend(7, qc // 2)
+        cols = pl.ds(256 * (qc % 2), 256)
+        out = acc[qc // 2, :, cols] * (1.0 / l_ref[qc // 2, :, cols])
         ob[pl.ds(32 * qc, 32)] = out.T.reshape(32, 8, 128)
         for t in (2 * (qc % 2) + 1, 2 * (qc % 2)):
             if qc < 2:
@@ -539,6 +585,17 @@
 
             got = do_ref.at[2 * g + p // 2, :, rows, :]
             pltpu.make_async_copy(got, got, sem_do_r.at[4 * t + g]).wait()
+
+
+def hand_over(here, also_here, there, also_there, held, also_held, sem_in, sem_out):
+    ends = ((here, held, there), (also_here, also_held, also_there))
+    for n, (src, mid, dst) in enumerate(ends):
+        pltpu.make_async_copy(src, mid, sem_in.at[n]).start()
+    for n, (src, mid, dst) in enumerate(ends):
+        pltpu.make_async_copy(src, mid, sem_in.at[n]).wait()
+        pltpu.make_async_copy(mid, dst, sem_out.at[n]).start()
+    for n, (src, mid, dst) in enumerate(ends):
+        pltpu.make_async_copy(mid, dst, sem_out.at[n]).wait()
 
 
 def on_device(kv_cache, prefill_q, decode_q, decode_kv, lengths, row_length):
@@ -568,13 +625,13 @@
             pltpu.VMEM((128, 8, 128), F32),
             pltpu.VMEM((16, 1, 128), jnp.int32),
             pltpu.VMEM((16, 8, 128), F32),
-            pltpu.VMEM((NQ, 768), BF16),
-            pltpu.VMEM((2, BLK, 768), BF16),
-            pltpu.VMEM((2, 256, BLK), BF16),
-            pltpu.VMEM((1, NQ), jnp.int32),
-            pltpu.VMEM((1, NQ), F32),
-            pltpu.VMEM((1, NQ), F32),
-            pltpu.VMEM((128, NQ), F32),
+            pltpu.VMEM((2, HALF, 768), BF16),
+            pltpu.VMEM((8, 2, BLK, 768), BF16),
+            pltpu.VMEM((8, 2, 256, BLK), BF16),
+            pltpu.VMEM((2, 1, HALF), jnp.int32),
+            pltpu.VMEM((2, 1, HALF), F32),
+            pltpu.VMEM((2, 1, HALF), F32),
+            pltpu.VMEM((2, 128, HALF), F32),
             pltpu.VMEM((128, 8, 128), F32),
             dma((2,)),
             pltpu.SemaphoreType.REGULAR((3,)),
@@ -604,6 +661,14 @@
         decode_q.reshape(8, 4, 16, 128),
         decode_kv.reshape(128, 128),
     )
+    shapes = [prefill_out.shape, decode_out.shape]
+    prefill_out, decode_out = pl.pallas_call(
+        hand_over,
+        out_shape=[jax.ShapeDtypeStruct(shape, F32) for shape in shapes],
+        in_specs=[hbm] * 2,
+        out_specs=[hbm] * 2,
+        scratch_shapes=[pltpu.VMEM(shape, F32) for shape in shapes] + [dma((2,)), dma((2,))],
+    )(prefill_out, decode_out)
     return prefill_out, decode_out.reshape(decode_q.shape)
 
 

time: 80.7 us -> 77.1 us (0.955)
  local copies, waits for them, and re-layouts: 2.42 us -> 0 us
    pallas_call x1, Pallas kernels: 76.1 us -> 73.5 us  [on_device(): pl.pallas_call(functools.partial(kernel, scale, span), out_shape=(jax.Sha...]
    unnamed x4 -> x0, local copies, waits for them, and re-layouts: 2.42 us -> none
    pallas_call x0 -> x1, Pallas kernels: none -> 1.77 us  [on_device(): pl.pallas_call(hand_over, out_shape=[jax.ShapeDtypeStruct(shape, F32) for...]
where the time goes in v3:
time: 77.1 us; the launch traced here: 76 us
  Pallas kernels  75.3 us (98%)
    pallas_call x1, Pallas kernels, on_device(): pl.pallas_call(functools.partial(kernel, scale, span), out_shape=(jax.Sha...  73.5 us
    pallas_call x1, Pallas kernels, on_device(): pl.pallas_call(hand_over, out_shape=[jax.ShapeDtypeStruct(shape, F32) for...  1.77 us

profile of v3, /device:TPU:24, one launch (start us, length us, event | category | flops | bytes accessed | tf_op | source)
XLA Modules:
  0.0 76.0 jit_solution(12090903637775825148)
XLA Ops:
  0.6 73.5 %shard_map.77 = (f32[2,16,16,128]{3,2,1,0:T(8,128)}, f32[8,4,16,128]{3,2,1,0:T(8,128)}) custom-call(s32[8]{0:T(128)} %len_ref.1, s32[8]{0:T(128)} %bitcast.10, f32[2,2,512,128]{3,2,1,0:T(8,128)} %bitcast.7, f32[2,16,16,128]{3,2,1,0:T(8,128)} %pq_ref.1, f32[8,4,16,128]{3,2,1,0:T(8,128)} %bitcast.8, f32[128,128]{1,0:T(8,128)} %bitcast.9), custom_call_target="tpu_custom_call" | custom-call | tf_op jit(solution)/shard_map/pallas_call | solution.py:607
  74.2 1.8 %shard_map.78 = (f32[2,16,16,128]{3,2,1,0:T(8,128)}, f32[8,4,16,128]{3,2,1,0:T(8,128)}) custom-call(f32[2,16,16,128]{3,2,1,0:T(8,128)} %get-tuple-element.6.here, f32[8,4,16,128]{3,2,1,0:T(8,128)} %get-tuple-element.7.also_here), custom_call_target="tpu_custom_call" | custom-call | tf_op jit(solution)/shard_map/pallas_call | solution.py:665

commit v4 on v3

--- a/solution.py
+++ b/solution.py
@@ -218,8 +218,8 @@
             pltpu.make_async_remote_copy(
                 src,
                 dst,
-                sem_y_s.at[g, n],
-                sem_y_r.at[y, n],
+                sem_y_s.at[n],
+                sem_y_r.at[n],
                 device_id=(c, g, x),
                 device_id_type=MESH,
             )
@@ -231,7 +231,7 @@
     def y_keep():
         reqs = pl.ds(pl.multiple_of(2 * y, 2), 2)
         return [
-            pltpu.make_async_copy(src, dst, sem_y_r.at[y, n])
+            pltpu.make_async_copy(src, dst, sem_y_r.at[n])
             for n, (src, dst) in enumerate(
                 ((dq_ref.at[reqs], rq.at[y]), (dsend.at[reqs], rd.at[y]), (rlb.at[reqs], rr.at[y]))
             )
@@ -245,7 +245,7 @@
         if t == 0:
             return pltpu.make_async_copy(src, dst, sem_pq_r.at[0])
         return pltpu.make_async_remote_copy(
-            src, dst, sem_pq_s.at[t], sem_pq_r.at[t], device_id=(2 * zt + core, y, x), device_id_type=MESH
+            src, dst, sem_pq_s.at[0], sem_pq_r.at[0], device_id=(2 * zt + core, y, x), device_id_type=MESH
         )
 
     def dq_parts(t, h):
@@ -262,8 +262,8 @@
         return pltpu.make_async_remote_copy(
             part[0],
             part[1],
-            sem_dq_s.at[4 * t + h, n],
-            sem_dq_r.at[4 * t + x, n],
+            sem_dq_s.at[n],
+            sem_dq_r.at[n],
             device_id=(2 * dest(t) + core, y, h),
             device_id_type=MESH,
         )
@@ -276,21 +276,11 @@
 
                 @pl.when(x == h)
                 def _():
-                    pltpu.make_async_copy(part[0], part[1], sem_dq_r.at[4 * t + x, n]).start()
+                    pltpu.make_async_copy(part[0], part[1], sem_dq_r.at[n]).start()
 
                 @pl.when(x != h)
                 def _():
                     dq_remote(t, h, n, part).start()
-
-    def dq_wait_send(t, h):
-        for n, part in enumerate(dq_parts(t, h)):
-            if t:
-                dq_remote(t, h, n, part).wait_send()
-            else:
-
-                @pl.when(x != h)
-                def _():
-                    dq_remote(t, h, n, part).wait_send()
 
     def piece(h):
         return pl.ds(PIECE * h, PIECE)
@@ -300,7 +290,7 @@
         return pltpu.make_async_remote_copy(
             sendb.at[zt // 2, :, piece(h)],
             kvb.at[t, :, piece(h)],
-            sem_kp_s.at[t, h],
+            sem_kp_s.at[t],
             sem_k_r.at[t, h],
             device_id=(2 * zt + core, y, x),
             device_id_type=MESH,
@@ -310,7 +300,7 @@
         return pltpu.make_async_remote_copy(
             kvb.at[t, :, piece(h)],
             kvb.at[t + 4, :, piece(h)],
-            sem_kf_s.at[t, h],
+            sem_kf_s.at[t],
             sem_k_r.at[t + 4, h],
             device_id=(2 * mate + core, y, x),
             device_id_type=MESH,
@@ -320,7 +310,7 @@
         return pltpu.make_async_remote_copy(
             kvb.at[u, :, piece(h)],
             kvb.at[u + 8, :, piece(h)],
-            sem_kx_s.at[u, h],
+            sem_kx_s.at[u],
             sem_k_r.at[u + 8, h],
             device_id=(2 * z + 1 - core, y, x),
             device_id_type=MESH,
@@ -355,9 +345,8 @@
                     copy.start()
 
     def along_y_done():
-        for g in range(4):
-            for n, part in enumerate((rq.at[g], rd.at[g], rr.at[g])):
-                pltpu.make_async_copy(part, part, sem_y_r.at[g, n]).wait()
+        for n, part in enumerate((rq, rd, rr)):
+            pltpu.make_async_copy(part, part, sem_y_r.at[n]).wait()
 
     def own_slot(m):
         slot = OWN[-1]
@@ -378,21 +367,16 @@
             q6[part, pl.ds(pl.multiple_of(128 * n, 128), 128), :] = query_terms(q)
 
     def prefill_queries():
-        for t in range(4):
-            part = qb.at[pl.ds(16 * t, 16)]
-            pltpu.make_async_copy(part, part, sem_pq_r.at[t]).wait()
+        part = qb.at[pl.ds(0, 64)]
+        pltpu.make_async_copy(part, part, sem_pq_r.at[0]).wait()
         split_queries(0)
         m_ref[0] = jnp.full((1, HALF), NEG_FILL, F32)
         l_ref[0] = jnp.zeros((1, HALF), F32)
         acc[0] = jnp.zeros((128, HALF), F32)
 
     def decode_queries():
-        @pl.loop(0, 16)
-        def _(s):
-            part = qb.at[pl.ds(64 + 4 * s, 4)]
-            pltpu.make_async_copy(part, part, sem_dq_r.at[s, 0]).wait()
-            pltpu.make_async_copy(db.at[s], db.at[s], sem_dq_r.at[s, 1]).wait()
-            pltpu.make_async_copy(lb.at[s], lb.at[s], sem_dq_r.at[s, 2]).wait()
+        for n, part in enumerate((qb.at[pl.ds(64, 64)], db, lb)):
+            pltpu.make_async_copy(part, part, sem_dq_r.at[n]).wait()
 
         for v in range(4):
             row = jnp.where(
@@ -484,9 +468,13 @@
     def _(m):
         send_on(m, 0)
         ready(m)
-        attend(m, 0)
+        attend(m, 1)
         send_on(m, 1)
-        attend(m, 1)
+
+        @pl.when(m % 2 == 1)
+        def _():
+            attend((m + 3) // 2, 0)
+
         send_on(m, 2)
 
     rows_j = pl.ds(pl.multiple_of(8 * own_j, 8), 8)
@@ -499,8 +487,8 @@
         return pltpu.make_async_remote_copy(
             src,
             dst,
-            sem_po_s.at[t],
-            sem_po_r.at[t],
+            sem_po_s.at[0],
+            sem_po_r.at[0],
             device_id=(2 * source_of(z, t) + core, y, x),
             device_id_type=MESH,
         )
@@ -513,8 +501,8 @@
         return pltpu.make_async_remote_copy(
             src,
             dst,
-            sem_do_s.at[4 * t + r],
-            sem_do_r.at[4 * t + y],
+            sem_do_s.at[4 if t else r],
+            sem_do_r.at[0],
             device_id=(2 * source_of(z, t) + core, x, r),
             device_id_type=MESH,
         )
@@ -528,7 +516,7 @@
         @pl.when(mine)
         def _():
             src, dst = do_ends(t, r)
-            pltpu.make_async_copy(src, dst, sem_do_r.at[4 * t + y]).start()
+            pltpu.make_async_copy(src, dst, sem_do_r.at[0]).start()
 
         @pl.when(jnp.logical_not(mine))
         def _():
@@ -536,8 +524,14 @@
 
     ready(7)
     for qc in (3, 2, 1, 0):
-        if qc % 2:
-            attend(7, qc // 2)
+        if qc == 3:
+            attend(7, 1)
+        elif qc == 1:
+
+            @pl.loop(5, 8)
+            def _(m):
+                attend(m, 0)
+
         cols = pl.ds(256 * (qc % 2), 256)
         out = acc[qc // 2, :, cols] * (1.0 / l_ref[qc // 2, :, cols])
         ob[pl.ds(32 * qc, 32)] = out.T.reshape(32, 8, 128)
@@ -548,43 +542,30 @@
                 for r in range(4):
                     do_start(t, r)
 
-    for g in range(4):
-
-        @pl.when(y != g)
-        def _():
-            for copy in y_copies(g):
-                copy.wait_send()
-
-    for t in range(1, 4):
-        pq_copy(t).wait_send()
-    for t in range(4):
-        for g in range(4):
-            dq_wait_send(t, g)
-        for h in range(PIECES):
-            if t:
-                kv_primary(t, h).wait_send()
-            kv_forward(t, h).wait_send()
-    for u in range(8):
-        for h in range(PIECES):
-            kv_cross(u, h).wait_send()
+    def ended(part, sem):
+        pltpu.make_async_copy(part, part, sem).wait()
+
+    for n, part in enumerate((rq, rd, rr)):
+        ended(part.at[pl.ds(0, 3)], sem_y_s.at[n])
+    ended(qb.at[pl.ds(0, 48)], sem_pq_s.at[0])
+    for n, part in enumerate((qb.at[pl.ds(0, 60)], db.at[pl.ds(0, 15)], lb.at[pl.ds(0, 15)])):
+        ended(part, sem_dq_s.at[n])
     for t in range(4):
         if t:
-            po_copy(t).wait_send()
-        p = dest(t) // 2
-        rows = pl.ds(pl.multiple_of(8 * (p % 2), 8), 8)
-        got = po_ref.at[p // 2, :, rows, :]
-        pltpu.make_async_copy(got, got, sem_po_r.at[t]).wait()
-        for g in range(4):
-            if t:
-                do_remote(t, g).wait_send()
-            else:
-
-                @pl.when(jnp.logical_not((x == g) & diag))
-                def _():
-                    do_remote(t, g).wait_send()
-
-            got = do_ref.at[2 * g + p // 2, :, rows, :]
-            pltpu.make_async_copy(got, got, sem_do_r.at[4 * t + g]).wait()
+            ended(kvb.at[t], sem_kp_s.at[t])
+        ended(kvb.at[t], sem_kf_s.at[t])
+    for u in range(8):
+        ended(kvb.at[u], sem_kx_s.at[u])
+    ended(ob.at[pl.ds(0, 48)], sem_po_s.at[0])
+    for r in range(4):
+
+        @pl.when(jnp.logical_not((x == r) & diag))
+        def _():
+            do_remote(0, r).wait_send()
+
+    ended(ob.at[pl.ds(80, 48)], sem_do_s.at[4])
+    ended(po_ref, sem_po_r.at[0])
+    ended(do_ref, sem_do_r.at[0])
 
 
 def hand_over(here, also_here, there, also_there, held, also_held, sem_in, sem_out):
@@ -635,20 +616,20 @@
             pltpu.VMEM((128, 8, 128), F32),
             dma((2,)),
             pltpu.SemaphoreType.REGULAR((3,)),
-            dma((4, 3)),
-            dma((4, 3)),
+            dma((3,)),
+            dma((3,)),
+            dma((1,)),
+            dma((1,)),
+            dma((3,)),
+            dma((3,)),
             dma((4,)),
             dma((4,)),
-            dma((16, 3)),
-            dma((16, 3)),
-            dma((4, PIECES)),
-            dma((4, PIECES)),
-            dma((8, PIECES)),
+            dma((8,)),
             dma((16, PIECES)),
-            dma((4,)),
-            dma((4,)),
-            dma((16,)),
-            dma((16,)),
+            dma((1,)),
+            dma((1,)),
+            dma((5,)),
+            dma((1,)),
         ],
         compiler_params=pltpu.CompilerParams(
             collective_id=0, has_side_effects=True, vmem_limit_bytes=56 * 1024 * 1024

time: 77.1 us -> 75.2 us (0.975)
  Pallas kernels: 75.3 us -> 73.6 us
    pallas_call x1, Pallas kernels: 73.5 us -> 71.8 us  [on_device(): pl.pallas_call(functools.partial(kernel, scale, span), out_shape=(jax.Sha...]
where the time goes in v4:
time: 75.2 us; the launch traced here: 74.2 us
  Pallas kernels  73.6 us (98%)
    pallas_call x1, Pallas kernels, on_device(): pl.pallas_call(functools.partial(kernel, scale, span), out_shape=(jax.Sha...  71.8 us
    pallas_call x1, Pallas kernels, on_device(): pl.pallas_call(hand_over, out_shape=[jax.ShapeDtypeStruct(shape, F32) for...  1.77 us

profile of v4, /device:TPU:24, one launch (start us, length us, event | category | flops | bytes accessed | tf_op | source)
XLA Modules:
  0.0 74.2 jit_solution(10629822720579575110)
XLA Ops:
  0.6 71.8 %shard_map.77 = (f32[2,16,16,128]{3,2,1,0:T(8,128)}, f32[8,4,16,128]{3,2,1,0:T(8,128)}) custom-call(s32[8]{0:T(128)} %len_ref.1, s32[8]{0:T(128)} %bitcast.10, f32[2,2,512,128]{3,2,1,0:T(8,128)} %bitcast.7, f32[2,16,16,128]{3,2,1,0:T(8,128)} %pq_ref.1, f32[8,4,16,128]{3,2,1,0:T(8,128)} %bitcast.8, f32[128,128]{1,0:T(8,128)} %bitcast.9), custom_call_target="tpu_custom_call" | custom-call | tf_op jit(solution)/shard_map/pallas_call | solution.py:588
  72.5 1.8 %shard_map.78 = (f32[2,16,16,128]{3,2,1,0:T(8,128)}, f32[8,4,16,128]{3,2,1,0:T(8,128)}) custom-call(f32[2,16,16,128]{3,2,1,0:T(8,128)} %get-tuple-element.6.here, f32[8,4,16,128]{3,2,1,0:T(8,128)} %get-tuple-element.7.also_here), custom_call_target="tpu_custom_call" | custom-call | tf_op jit(solution)/shard_map/pallas_call | solution.py:646

commit v5 on v4

--- a/solution.py
+++ b/solution.py
@@ -17,7 +17,7 @@
 BLK = 256
 PIECES = 2
 PIECE = BLK // PIECES
-OWN = (0, 4, 1, 5, 3, 2, 7, 6)
+OWN = (0, 4, 1, 5, 2, 3, 6, 7)
 SPOT = (1, 1)
 PLAN = (
     ("y", 0),
@@ -55,14 +55,14 @@
     ("arrive", (2, 1)),
     ("ready", 2),
     ("attend", (2, 0)),
-    ("arrive", (5, 0)),
+    ("arrive", (4, 0)),
     ("decode queries", 0),
     ("attend", (0, 1)),
     ("attend", (1, 1)),
     ("arrive", (3, 0)),
     ("arrive", (3, 1)),
     ("attend", (2, 1)),
-    ("arrive", (4, 0)),
+    ("arrive", (5, 0)),
 )
 EARLY = 1 + max(which for what, which in PLAN if what == "ready")
 

time: 75.2 us -> 73.4 us (0.976)
  Pallas kernels: 73.6 us -> 72.2 us
    pallas_call x1, Pallas kernels: 71.8 us -> 70.4 us  [on_device(): pl.pallas_call(functools.partial(kernel, scale, span), out_shape=(jax.Sha...]
where the time goes in v5:
time: 73.4 us; the launch traced here: 72.8 us
  Pallas kernels  72.2 us (98%)
    pallas_call x1, Pallas kernels, on_device(): pl.pallas_call(functools.partial(kernel, scale, span), out_shape=(jax.Sha...  70.4 us
    pallas_call x1, Pallas kernels, on_device(): pl.pallas_call(hand_over, out_shape=[jax.ShapeDtypeStruct(shape, F32) for...  1.77 us

profile of v5, /device:TPU:24, one launch (start us, length us, event | category | flops | bytes accessed | tf_op | source)
XLA Modules:
  0.0 72.8 jit_solution(14127221949846044446)
XLA Ops:
  0.6 70.4 %shard_map.77 = (f32[2,16,16,128]{3,2,1,0:T(8,128)}, f32[8,4,16,128]{3,2,1,0:T(8,128)}) custom-call(s32[8]{0:T(128)} %len_ref.1, s32[8]{0:T(128)} %bitcast.10, f32[2,2,512,128]{3,2,1,0:T(8,128)} %bitcast.7, f32[2,16,16,128]{3,2,1,0:T(8,128)} %pq_ref.1, f32[8,4,16,128]{3,2,1,0:T(8,128)} %bitcast.8, f32[128,128]{1,0:T(8,128)} %bitcast.9), custom_call_target="tpu_custom_call" | custom-call | tf_op jit(solution)/shard_map/pallas_call | solution.py:588
  71.1 1.8 %shard_map.78 = (f32[2,16,16,128]{3,2,1,0:T(8,128)}, f32[8,4,16,128]{3,2,1,0:T(8,128)}) custom-call(f32[2,16,16,128]{3,2,1,0:T(8,128)} %get-tuple-element.6.here, f32[8,4,16,128]{3,2,1,0:T(8,128)} %get-tuple-element.7.also_here), custom_call_target="tpu_custom_call" | custom-call | tf_op jit(solution)/shard_map/pallas_call | solution.py:646
